TPU v7x, 128 devices: a whole 4x4x4 slice. The times are simulated.
128 devices in a mesh: gx: 4 (over z), gy: 4 (over x), gz: 8 (over y, core).
Axes of the slice: x: 4, y: 4, z: 4, core: 2. Of those that a mesh axis runs over, the one named last changes fastest.
Arguments:
- right_side: float32 [64, 64, 128, 256], P('gx', 'gy', 'gz'), may hold values from -35 to 35
- conductivity: float32 [64, 64, 128], P('gx', 'gy', 'gz'), may hold values from 0.25 to 2
- reaction: float32 [64, 64, 128], P('gx', 'gy', 'gz'), may hold values from 0.25 to 4
- leaf_factor: float32 [8, 8, 16, 512, 512], P('gx', 'gy', 'gz'), as said below
- leaf_weight: float32 [8, 8, 16, 512, 64], P('gx', 'gy', 'gz'), may hold values from -0.25 to 0.25
- leaf_skeleton: int32 [8, 8, 16, 64], P('gx', 'gy', 'gz'), may hold values from 0 to 511, as said below
- device_factor: float32 [4, 4, 8, 512, 512], P('gx', 'gy', 'gz'), as said below
- device_weight: float32 [4, 4, 8, 512, 256], P('gx', 'gy', 'gz'), may hold values from -0.25 to 0.25
- device_skeleton: int32 [4, 4, 8, 256], P('gx', 'gy', 'gz'), may hold values from 0 to 511, as said below
- column_factor: float32 [4, 4, 2048, 2048], P('gx', 'gy', 'gz'), as said below
- column_weight: float32 [4, 4, 2048, 128], P('gx', 'gy'), may hold values from -0.125 to 0.125
- column_skeleton: int32 [4, 4, 128], P('gx', 'gy'), may hold values from 0 to 2047, as said below
- top_factor: float32 [2048, 2048], P(('gx', 'gy')), as said below
Outputs:
- solution: float32 [64, 64, 128, 256], P('gx', 'gy', 'gz')
Inputs may be any that keep to these rules, and one draw needn't show every extreme that they name: `leaf_factor`: each box's block is symmetric and positive definite. `device_factor`: each domain block's block is symmetric and positive definite. `column_factor`: each column's block is symmetric and positive definite. `top_factor`: symmetric and positive definite. `leaf_skeleton`: the 64 numbers of one box are all different. `device_skeleton`: the 256 numbers of one domain block are all different. `column_skeleton`: the 128 numbers of one column are all different.
All inputs are finite; a program needn't handle non-finite values.
Results may differ from a plain program's by a relative error of at most 0.0001.
Values sent between devices are 32-bit elements; how exact they have to be, the bound alone decides.
A program may use at most 128 MiB of HBM per device.

v0:
```python
import jax
import jax.numpy as jnp
from jax import lax
from jax.experimental import pallas as pl
from jax.experimental.pallas import tpu as pltpu
from jax.sharding import PartitionSpec as P

F32, BF16 = jnp.float32, jnp.bfloat16
MESH = pl.DeviceIdType.MESH
B = 16
N = 256
NPQ, NS = 16, 8
PIECE = N // NS


def split(value):
    high = value.astype(BF16)
    return high, (value - high.astype(F32)).astype(BF16)


def mm(a, b):
    return jnp.dot(a, b, preferred_element_type=F32)


def mm_nt(a, b):
    return lax.dot_general(a, b, (((1,), (1,)), ((), ())), preferred_element_type=F32)


def dot3(a, b, product=mm):
    a_high, a_low = split(a)
    b_high, b_low = split(b)
    return product(a_high, b_high) + product(a_high, b_low) + product(a_low, b_high)


def each(first, count, body):
    def step(i, carry):
        body(i)
        return carry

    lax.fori_loop(first, count, step, 0)


def box_of(b, lead):
    x, y, z = lax.div(b, 4), lax.rem(lax.div(b, 2), 2), lax.rem(b, 2)
    return (
        pl.ds(8 * x + lead, 8),
        pl.ds(8 * y + lead, 8),
        pl.ds(pl.multiple_of(8 * z, 8), 8),
        slice(None),
    )


def kernel(
    rhs_hbm,
    half_hbm,
    react_hbm,
    leaf_hbm,
    leaf_v_hbm,
    dev_hbm,
    dev_v_hbm,
    col_hbm,
    col_v_hbm,
    top_hbm,
    out_hbm,
    rhs,
    half,
    react,
    leaf,
    leaf_hi,
    leaf_lo,
    leaf_v,
    leaf_vt,
    leaf_v3,
    dev,
    dev_v,
    dev_vt,
    col,
    col_v,
    col_vt,
    top,
    field,
    image,
    dev_in,
    dev_out,
    up_t,
    gath,
    rs,
    ag,
    tg,
    ar1,
    ar2,
    zsend,
    zrecv,
    hzsend,
    hzrecv,
    loc_sem,
    out_sem,
    gath_s,
    gath_r,
    rs_s,
    rs_r,
    ag_s,
    ag_r,
    tg_s,
    tg_r,
    a1_s,
    a1_r,
    a2_s,
    a2_r,
    halo_s,
    halo_r,
    hh_s,
    hh_r,
):
    gx, gy, gz = lax.axis_index("gx"), lax.axis_index("gy"), lax.axis_index("gz")
    pq = gx * 4 + gy
    chip, core = lax.div(gz, 2), lax.rem(gz, 2)
    mate = gz + 1 - 2 * core
    inner = pl.ds(1, B)

    def plane_id(peer):
        return {"gx": lax.div(peer, 4), "gy": lax.rem(peer, 4)}

    def local(i, src, dst):
        return pltpu.make_async_copy(src, dst, loc_sem.at[i])

    loads = [
        local(0, rhs_hbm, rhs),
        local(1, leaf_v_hbm, leaf_v),
        local(2, dev_v_hbm, dev_v),
        local(3, col_v_hbm, col_v),
        local(4, half_hbm, half.at[inner, inner]),
        local(5, dev_hbm, dev),
        local(6, top_hbm, top),
        local(7, col_hbm, col),
        local(8, react_hbm, react),
    ]
    leaf_loads = [local(9 + b, leaf_hbm.at[b], leaf.at[b]) for b in range(8)]
    for copy in loads[:4] + leaf_loads[:2] + loads[4:] + leaf_loads[2:]:
        copy.start()

    barrier = pltpu.get_barrier_semaphore()

    def greet_column(d):
        pl.semaphore_signal(
            barrier, inc=1, device_id={"gz": lax.rem(gz + d, NS)}, device_id_type=MESH
        )

    def greet_plane(d):
        pl.semaphore_signal(
            barrier, inc=1, device_id=plane_id(lax.rem(pq + d, NPQ)), device_id_type=MESH
        )

    each(1, NS, greet_column)
    each(1, NPQ, greet_plane)
    pl.semaphore_wait(barrier, NS - 1 + NPQ - 1)

    def remote(src, dst, send, recv, device):
        return pltpu.make_async_remote_copy(
            src_ref=src,
            dst_ref=dst,
            send_sem=send,
            recv_sem=recv,
            device_id=device,
            device_id_type=MESH,
        )

    def column_start(buf, send, recv, k):
        def body(d):
            peer = lax.rem(gz + d, NS)
            remote(
                buf.at[k, gz], buf.at[k, gz], send.at[k, peer], recv.at[k, gz], {"gz": peer}
            ).start()

        each(1, NS, body)

    def column_wait(buf, send, recv, k):
        def body(d):
            peer = lax.rem(gz + d, NS)
            remote(
                buf.at[k, gz], buf.at[k, peer], send.at[k, peer], recv.at[k, peer], {"gz": peer}
            ).wait()

        each(1, NS, body)

    def plane_start(buf, send, recv, k):
        def body(d):
            peer = lax.rem(pq + d, NPQ)
            remote(
                buf.at[k, pq], buf.at[k, pq], send.at[k, peer], recv.at[k, pq], plane_id(peer)
            ).start()

        each(1, NPQ, body)

    def plane_wait(buf, send, recv, k):
        def body(d):
            peer = lax.rem(pq + d, NPQ)
            remote(
                buf.at[k, pq], buf.at[k, peer], send.at[k, peer], recv.at[k, peer], plane_id(peer)
            ).wait()

        each(1, NPQ, body)

    sides = ((gx, 4, "gx"), (gy, 4, "gy"), (gz, NS, "gz"))

    def layers(array, zs, zr):
        return (
            ((array.at[B, inner], array.at[0, inner]), (array.at[1, inner], array.at[B + 1, inner])),
            ((array.at[inner, B], array.at[inner, 0]), (array.at[inner, 1], array.at[inner, B + 1])),
            ((zs.at[1], zr.at[0]), (zs.at[0], zr.at[1])),
        )

    def halo_copies(array, zs, zr, send, recv):
        copies = []
        for axis, ((place, extent, name), pairs) in enumerate(zip(sides, layers(array, zs, zr))):
            for way, (src, dst) in enumerate(pairs):
                there = place + 1 if way == 0 else place - 1
                exists = place < extent - 1 if way == 0 else place > 0
                arrives = place > 0 if way == 0 else place < extent - 1
                i = 2 * axis + way
                copies.append(
                    (remote(src, dst, send.at[i], recv.at[i], {name: there}), exists, arrives, dst)
                )
        return copies

    def halo_start(copies):
        for copy, exists, _, _ in copies:
            pl.when(exists)(copy.start)

    def halo_zero(copies):
        for _, _, arrives, dst in copies:

            @pl.when(jnp.logical_not(arrives))
            def _():
                dst[...] = jnp.zeros(dst.shape, F32)

    def halo_wait(copies):
        for copy, exists, arrives, _ in copies:
            pl.when(exists)(copy.wait_send)
            pl.when(arrives)(copy.wait_recv)

    def pack_z(array, zs):
        def body(x):
            zs[0, x] = array[x + 1, 1 : B + 1, 0, :]
            zs[1, x] = array[x + 1, 1 : B + 1, B - 1, :]

        each(0, B, body)

    hh = halo_copies(half, hzsend, hzrecv, hh_s, hh_r)
    halos = [
        halo_copies(field.at[k], zsend.at[k], zrecv.at[k], halo_s.at[k], halo_r.at[k])
        for k in range(2)
    ]

    def restrict_all(src, k):
        def leaf_box(b):
            u_high, u_low = split(src[box_of(b, 0)].reshape(512, N))
            both = mm(leaf_vt[b], u_high)
            total = both[:64] + both[64:] + mm(leaf_vt[b, :64], u_low)
            dev_in[pl.ds(pl.multiple_of(b * 64, 64), 64), :] = total

        each(0, 8, leaf_box)
        device_up = dot3(dev_vt[...], dev_in[...])
        gath[k, gz] = device_up
        up_t[k] = dot3(col_vt[...], device_up).T
        rs[k, gz] = up_t[k, pl.ds(pl.multiple_of(gz * PIECE, PIECE), PIECE), :]

    def rs_start(k):
        def body(d):
            peer = lax.rem(gz + d, NS)
            remote(
                up_t.at[k, pl.ds(pl.multiple_of(peer * PIECE, PIECE), PIECE)],
                rs.at[k, gz],
                rs_s.at[k, peer],
                rs_r.at[k, gz],
                {"gz": peer},
            ).start()

        each(1, NS, body)

    def rs_wait(k):
        def body(d):
            peer = lax.rem(gz + d, NS)
            remote(
                up_t.at[k, pl.ds(pl.multiple_of(peer * PIECE, PIECE), PIECE)],
                rs.at[k, peer],
                rs_s.at[k, peer],
                rs_r.at[k, peer],
                {"gz": peer},
            ).wait()

        each(1, NS, body)

    def gath_copies(k):
        direct = [
            remote(gath.at[k, gz], gath.at[k, gz], gath_s.at[k, 0], gath_r.at[k, gz], {"gz": mate})
        ]
        passed, arrivals = [], []
        for i, j in enumerate((1, 3, 2)):
            peer = lax.rem(chip + j, 4) * 2 + core
            direct.append(
                remote(
                    gath.at[k, gz],
                    gath.at[k, gz],
                    gath_s.at[k, 1 + i],
                    gath_r.at[k, gz],
                    {"gz": peer},
                )
            )
            back = lax.rem(chip + j, 4) * 2 + core
            arrivals.append(
                remote(
                    gath.at[k, back],
                    gath.at[k, back],
                    gath_s.at[k, 4 + i],
                    gath_r.at[k, back],
                    {"gz": mate},
                )
            )
            other = lax.rem(chip + j, 4) * 2 + 1 - core
            passed.append(
                remote(
                    gath.at[k, other],
                    gath.at[k, other],
                    gath_s.at[k, 4 + i],
                    gath_r.at[k, other],
                    {"gz": mate},
                )
            )
        from_mate = remote(
            gath.at[k, mate], gath.at[k, mate], gath_s.at[k, 0], gath_r.at[k, mate], {"gz": mate}
        )
        return direct, arrivals, passed, from_mate

    def leaf_products(src, k, first, last):
        def body(b):
            u_high, u_low = split(src[box_of(b, 0)].reshape(512, N))
            if k == 0:
                pltpu.make_async_copy(leaf_hbm.at[b], leaf.at[b], loc_sem.at[9 + b]).wait()
                high, low = split(leaf[b])
                leaf_hi[b] = high
                leaf_lo[b] = low
            else:
                high, low = leaf_hi[b], leaf_lo[b]
            total = mm(high, u_high) + mm(high, u_low) + mm(low, u_high)
            field[(k,) + box_of(b, 1)] = total.reshape(8, 8, 8, N)

        each(first, last, body)

    def precondition(src, k, middle, last_step):
        restrict_all(src, k)
        rs_start(k)
        direct, arrivals, passed, from_mate = gath_copies(k)
        for copy in direct:
            copy.start()
        middle()
        leaf_products(src, k, 0, 3)
        rs_wait(k)
        total = rs[k, 0]
        for i in range(1, NS):
            total = total + rs[k, i]
        ag[k, pq] = total
        plane_start(ag, ag_s, ag_r, k)
        leaf_products(src, k, 3, 6)
        plane_wait(ag, ag_s, ag_r, k)
        if k == 0:
            loads[6].wait()
        tops = jnp.concatenate([ag[k, i] for i in range(NPQ)], axis=1)
        tg[k, gz] = dot3(tops, top[...], mm_nt)
        column_start(tg, tg_s, tg_r, k)
        for copy in arrivals:
            copy.wait_recv()
            copy.start()
        leaf_products(src, k, 6, 8)
        if k == 0:
            loads[5].wait()
            loads[7].wait()
        dev_out[...] = dot3(dev[...], dev_in[...])
        from_mate.wait_recv()
        for copy in passed:
            copy.wait_recv()
        near = dot3(col[...], gath[k].reshape(NS * 256, N))
        column_wait(tg, tg_s, tg_r, k)
        column_out = near + dot3(col_v[...], tg[k].reshape(N, 128), mm_nt)
        dev_out[...] += dot3(dev_v[...], column_out)
        for copy in direct + arrivals:
            copy.wait_send()
        last_step()

    def lift_boxes(k, finish):
        def body(b):
            high, low = split(dev_out[pl.ds(pl.multiple_of(b * 64, 64), 64), :])
            stacked = jnp.concatenate([high, low, high, jnp.zeros_like(high)], axis=0)
            place = (k,) + box_of(b, 1)
            total = field[place].reshape(512, N) + mm(leaf_v3[b], stacked)
            finish(b, place, total.reshape(8, 8, 8, N))

        each(0, 8, body)

    def stencil(k, use):
        rows = lax.broadcasted_iota(jnp.int32, (B, N), 0)
        first, last = rows == 0, rows == B - 1
        first_h, last_h = first[:, :128], last[:, :128]

        def shifted(value, low, high, is_first, is_last):
            up = jnp.where(is_last, high, pltpu.roll(value, B - 1, 0))
            down = jnp.where(is_first, low, pltpu.roll(value, 1, 0))
            return up, down

        def body(x, carry):
            energy, curve = carry
            for y in range(B):
                v = field[k, x + 1, y + 1]
                h = half[x + 1, y + 1]
                v_up, v_down = shifted(
                    v, zrecv[k, 0, x, y : y + 1, :], zrecv[k, 1, x, y : y + 1, :], first, last
                )
                h_up, h_down = shifted(
                    h, hzrecv[0, x, y : y + 1, :], hzrecv[1, x, y : y + 1, :], first_h, last_h
                )
                total = react[x, y]
                pairs = (
                    (half[x, y + 1], field[k, x, y + 1]),
                    (half[x + 2, y + 1], field[k, x + 2, y + 1]),
                    (half[x + 1, y], field[k, x + 1, y]),
                    (half[x + 1, y + 2], field[k, x + 1, y + 2]),
                    (h_up, v_up),
                    (h_down, v_down),
                )
                off = None
                for other, value in pairs:
                    face = h + other
                    total = total + face
                    part = jnp.concatenate([face, face], axis=1) * value
                    off = part if off is None else off + part
                applied = jnp.concatenate([total, total], axis=1) * v - off
                residual = use(x, y, applied)
                energy = energy + residual * v
                curve = curve + v * applied
            return energy, curve

        zero = jnp.zeros((B, N), F32)
        return lax.fori_loop(0, B, body, (zero, zero))

    def ar_first(k, energy, curve):
        row = lax.broadcasted_iota(jnp.int32, (8, N), 0)
        e = jnp.sum(energy, axis=0, keepdims=True)
        c = jnp.sum(curve, axis=0, keepdims=True)
        ar1[k, gz] = jnp.where(row == 0, e, jnp.where(row == 1, c, 0.0))
        column_start(ar1, a1_s, a1_r, k)

    def ar_second(k):
        column_wait(ar1, a1_s, a1_r, k)
        total = ar1[k, 0]
        for i in range(1, NS):
            total = total + ar1[k, i]
        ar2[k, pq] = total
        plane_start(ar2, a2_s, a2_r, k)

    def ar_third(k):
        plane_wait(ar2, a2_s, a2_r, k)
        total = ar2[k, 0]
        for i in range(1, NPQ):
            total = total + ar2[k, i]
        return total[0:1], total[1:2]

    loads[1].wait()

    def prepare(b):
        high, low = split(leaf_v[b])
        leaf_vt[b] = jnp.concatenate([high, low], axis=0)
        high, low = high.astype(F32), low.astype(F32)
        leaf_v3[b] = jnp.concatenate([high, high, low, jnp.zeros_like(low)], axis=0).T.astype(BF16)

    each(0, 8, prepare)
    loads[2].wait()
    dev_vt[...] = dev_v[...].T
    loads[3].wait()
    col_vt[...] = col_v[...].T
    loads[0].wait()

    for copies in [hh] + halos:
        halo_zero(copies)

    def send_halves():
        loads[4].wait()
        pack_z(half, hzsend)
        halo_start(hh)

    precondition(rhs, 0, send_halves, lambda: None)

    def keep(b, place, total):
        field[place] = total

    lift_boxes(0, keep)
    pack_z(field.at[0], zsend.at[0])
    halo_start(halos[0])
    halo_wait(hh)
    loads[8].wait()
    halo_wait(halos[0])

    def use_first(x, y, applied):
        image[x, y] = applied
        return rhs[x, y]

    energy, curve = stencil(0, use_first)
    ar_first(0, energy, curve)

    precondition(image, 1, lambda: None, lambda: None)
    ar_second(0)
    energy0, curve0 = ar_third(0)
    step0 = energy0 / curve0

    def subtract(b, place, total):
        field[place] = field[(0,) + place[1:]] - step0.reshape(1, 1, 1, N) * total

    lift_boxes(1, subtract)
    pack_z(field.at[1], zsend.at[1])
    halo_start(halos[1])
    halo_wait(halos[1])

    def use_second(x, y, applied):
        return rhs[x, y] - step0 * image[x, y]

    energy, curve = stencil(1, use_second)
    ar_first(1, energy, curve)
    ar_second(1)
    energy1, curve1 = ar_third(1)
    mixing = energy1 / energy0
    step1 = energy1 / (curve1 - mixing * energy1 / step0)
    ahead = (step0 + step1 * mixing).reshape(1, 1, N)
    last = step1.reshape(1, 1, N)

    def write(x):
        image[x] = ahead * field[0, x + 1, 1 : B + 1] + last * field[1, x + 1, 1 : B + 1]
        pltpu.make_async_copy(image.at[x], out_hbm.at[x], out_sem.at[x]).start()

    each(0, B, write)

    def written(x):
        pltpu.make_async_copy(image.at[x], out_hbm.at[x], out_sem.at[x]).wait()

    each(0, B, written)


def local(
    right_side,
    conductivity,
    reaction,
    leaf_factor,
    leaf_weight,
    leaf_skeleton,
    device_factor,
    device_weight,
    device_skeleton,
    column_factor,
    column_weight,
    column_skeleton,
    top_factor,
):
    def onehot(skeleton, rows, first=0):
        numbers = lax.broadcasted_iota(jnp.int32, (rows, 1), 0) + first
        return (numbers == skeleton[None, :]).astype(F32)

    wide = (B, B, B, 128)
    half = jnp.broadcast_to((0.5 * conductivity)[..., None], wide)
    react = jnp.broadcast_to(reaction[..., None], wide)
    skeleton = leaf_skeleton.reshape(8, 64)
    leaf_v = jnp.swapaxes(leaf_weight.reshape(8, 512, 64), 1, 2) + (
        skeleton[..., None] == lax.broadcasted_iota(jnp.int32, (1, 1, 512), 2)
    ).astype(F32)
    dev_v = device_weight[0, 0, 0] + onehot(device_skeleton[0, 0, 0], 512)
    start = lax.axis_index("gz") * 256
    col_v = lax.dynamic_slice_in_dim(column_weight[0, 0], start, 256, 0) + onehot(
        column_skeleton[0, 0], 256, start
    )
    any_space = pl.BlockSpec(memory_space=pl.ANY)
    dma = pltpu.SemaphoreType.DMA
    vm = pltpu.VMEM
    scratch = [
        vm((B, B, B, N), F32),
        vm((B + 2, B + 2, B, 128), F32),
        vm((B, B, B, 128), F32),
        vm((8, 512, 512), F32),
        vm((8, 512, 512), BF16),
        vm((8, 512, 512), BF16),
        vm((8, 64, 512), F32),
        vm((8, 128, 512), BF16),
        vm((8, 512, 256), BF16),
        vm((512, 512), F32),
        vm((512, 256), F32),
        vm((256, 512), F32),
        vm((256, 2048), F32),
        vm((256, 128), F32),
        vm((128, 256), F32),
        vm((128, 2048), F32),
        vm((2, B + 2, B + 2, B, N), F32),
        vm((B, B, B, N), F32),
        vm((512, N), F32),
        vm((512, N), F32),
        vm((2, N, 128), F32),
        vm((2, NS, 256, N), F32),
        vm((2, NS, PIECE, 128), F32),
        vm((2, NPQ, PIECE, 128), F32),
        vm((2, NS, PIECE, 128), F32),
        vm((2, NS, 8, N), F32),
        vm((2, NPQ, 8, N), F32),
        vm((2, 2, B, B, N), F32),
        vm((2, 2, B, B, N), F32),
        vm((2, B, B, 128), F32),
        vm((2, B, B, 128), F32),
        dma((17,)),
        dma((B,)),
        dma((2, NS)),
        dma((2, NS)),
        dma((2, NS)),
        dma((2, NS)),
        dma((2, NPQ)),
        dma((2, NPQ)),
        dma((2, NS)),
        dma((2, NS)),
        dma((2, NS)),
        dma((2, NS)),
        dma((2, NPQ)),
        dma((2, NPQ)),
        dma((2, 6)),
        dma((2, 6)),
        dma((6,)),
        dma((6,)),
    ]
    return pl.pallas_call(
        kernel,
        out_shape=jax.ShapeDtypeStruct((B, B, B, N), F32),
        in_specs=[any_space] * 10,
        out_specs=any_space,
        scratch_shapes=scratch,
        compiler_params=pltpu.CompilerParams(
            collective_id=0, has_side_effects=True, vmem_limit_bytes=67043328
        ),
        name="cg",
    )(
        right_side,
        half,
        react,
        leaf_factor.reshape(8, 512, 512),
        leaf_v,
        device_factor[0, 0, 0],
        dev_v,
        column_factor[0, 0],
        col_v,
        top_factor,
    )


def solution(mesh):
    cells = P("gx", "gy", "gz")
    in_specs = (cells,) * 10 + (P("gx", "gy"), P("gx", "gy"), P(("gx", "gy"), None))
    return jax.shard_map(local, mesh=mesh, in_specs=in_specs, out_specs=cells, check_vma=False)
```

profile of v0, /device:TPU:1, one launch (start us, length us, event | category | flops | bytes accessed | tf_op | source)
XLA Modules:
  0.0 115.4 jit_solution(9232090980427737647)
XLA Ops:
  0.0 0.0 copy-start
  0.0 1.7 %bitcast_add_fusion.2.col_v_hbm = f32[256,128]{1,0:T(8,128)} fusion(f32[1,1,2048,128]{3,2,1,0:T(8,128)} %param.23, s32[]{:T(128)S(6)} %select_n.3, s32[128]{0:T(128)} %bitcast.19, s32[256]{0:T(256)S(1)} %iota_add_fusion), kind=kLoop, calls=%fused_computation.4 | loop fusion | flops 98304 | bytes 263684 | tf_op jit(solution)/shard_map/add | solution.py:574
  1.7 0.9 broadcast_multiply_fusion
  2.6 1.9 %bitcast_add_fusion.1.dev_v_hbm = f32[512,256]{1,0:T(8,128)} fusion(f32[1,1,1,512,256]{4,3,2,1,0:T(8,128)} %param.20, s32[256]{0:T(256)} %bitcast.18), kind=kLoop, calls=%fused_computation.2 | loop fusion | flops 393216 | bytes 1049600 | tf_op jit(solution)/shard_map/add | solution.py:572
  4.5 2.4 %bitcast_add_fusion.leaf_v_hbm = f32[8,64,512]{2,1,0:T(8,128)} fusion(f32[2,2,2,512,64]{3,4,2,1,0:T(8,128)} %param.17, s32[8,64]{1,0:T(8,128)} %bitcast.17), kind=kLoop, calls=%fused_computation | loop fusion | flops 786432 | bytes 2099200 | tf_op jit(solution)/shard_map/add | solution.py:569
  6.9 1.9 %broadcast_in_dim.4.half_hbm = f32[16,16,16,128]{3,2,1,0:T(8,128)} broadcast(f32[16,16,16]{2,1,0:T(8,128)S(1)} %broadcast_multiply_fusion), dimensions={0,1,2} | broadcast | bytes 2113536 | tf_op jit(solution)/shard_map/broadcast_in_dim | solution.py:566
  8.8 0.0 copy-done
  8.8 1.9 %broadcast_in_dim.5.react_hbm = f32[16,16,16,128]{3,2,1,0:T(8,128)} broadcast(f32[16,16,16]{2,1,0:T(8,128)S(1)} %copy-done), dimensions={0,1,2} | broadcast | bytes 2113536 | tf_op jit(solution)/shard_map/broadcast_in_dim | solution.py:567
  10.8 99.8 %cg.1 = f32[16,16,16,256]{3,2,1,0:T(8,128)} custom-call(f32[16,16,16,256]{3,2,1,0:T(8,128)} %rhs_hbm.1, f32[16,16,16,128]{3,2,1,0:T(8,128)} %broadcast_in_dim.4.half_hbm, f32[16,16,16,128]{3,2,1,0:T(8,128)} %broadcast_in_dim.5.react_hbm, f32[8,512,512]{2,1,0:T(8,128)} %bitcast.14, f32[8,64,512]{2,1,0:T(8,128)} %bitcast_add_fusion.leaf_v_hbm, ...), custom_call_target="tpu_custom_call" | custom-call | tf_op jit(solution)/shard_map/cg/pallas_call | solution.py:631
  110.6 4.8 %copy.15 = f32[16,16,16,256]{3,2,1,0:T(8,128)} copy(f32[16,16,16,256]{3,2,1,0:T(8,128)} %cg.1) | data formatting | bytes 8388608
  (1 shorter events, 0.0 us)
Async XLA Ops:
  0.0 8.8 %copy-start = (f32[16,16,16]{2,1,0:T(8,128)S(1)}, f32[16,16,16]{2,1,0:T(8,128)}, u32[]{:S(2)}) copy-start(f32[16,16,16]{2,1,0:T(8,128)} %param.15) | copy-start | bytes 49156
where the time goes:
time: 116 us; the launch traced here: 115 us
  Pallas kernels  99.8 us (86%)
  local copies, waits for them, and re-layouts  8.66 us (7%)
  other arithmetic  6.9 us (6%)
    pallas_call x1, Pallas kernels, local(): pl.pallas_call(kernel, out_shape=jax.ShapeDtypeStruct((B, B, B, N), F32),...  99.8 us
    unnamed x3, local copies, waits for them, and re-layouts  4.81 us
    add x1, other arithmetic, local(): jnp.swapaxes(leaf_weight.reshape(8, 512, 64), 1, 2)  2.4 us

commit v1 on v0

--- a/solution.py
+++ b/solution.py
@@ -52,17 +52,25 @@
 
 def kernel(
     rhs_hbm,
-    half_hbm,
+    cond_hbm,
     react_hbm,
     leaf_hbm,
-    leaf_v_hbm,
+    leaf_w_hbm,
+    leaf_s_hbm,
     dev_hbm,
-    dev_v_hbm,
+    dev_w_hbm,
+    dev_s_hbm,
     col_hbm,
-    col_v_hbm,
+    col_w_hbm,
+    col_s_hbm,
     top_hbm,
     out_hbm,
     rhs,
+    cond_raw,
+    react_raw,
+    leaf_s,
+    dev_s,
+    col_s,
     half,
     react,
     leaf,
@@ -84,6 +92,7 @@
     dev_out,
     up_t,
     gath,
+    near,
     rs,
     ag,
     tg,
@@ -126,17 +135,20 @@
 
     loads = [
         local(0, rhs_hbm, rhs),
-        local(1, leaf_v_hbm, leaf_v),
-        local(2, dev_v_hbm, dev_v),
-        local(3, col_v_hbm, col_v),
-        local(4, half_hbm, half.at[inner, inner]),
+        local(1, leaf_w_hbm, leaf_v),
+        local(2, dev_w_hbm, dev_v),
+        local(3, col_w_hbm.at[pl.ds(pl.multiple_of(gz * 256, 256), 256)], col_v),
+        local(4, cond_hbm, cond_raw),
         local(5, dev_hbm, dev),
         local(6, top_hbm, top),
         local(7, col_hbm, col),
-        local(8, react_hbm, react),
+        local(8, react_hbm, react_raw),
+        local(17, leaf_s_hbm, leaf_s),
+        local(18, dev_s_hbm, dev_s),
+        local(19, col_s_hbm, col_s),
     ]
-    leaf_loads = [local(9 + b, leaf_hbm.at[b], leaf.at[b]) for b in range(8)]
-    for copy in loads[:4] + leaf_loads[:2] + loads[4:] + leaf_loads[2:]:
+    leaf_loads = [local(9 + b, leaf_hbm.at[b], leaf.at[b]) for b in range(4)]
+    for copy in loads[9:] + loads[1:4] + loads[:1] + leaf_loads[:2] + loads[4:9] + leaf_loads[2:]:
         copy.start()
 
     barrier = pltpu.get_barrier_semaphore()
@@ -153,8 +165,6 @@
 
     each(1, NS, greet_column)
     each(1, NPQ, greet_plane)
-    pl.semaphore_wait(barrier, NS - 1 + NPQ - 1)
-
     def remote(src, dst, send, recv, device):
         return pltpu.make_async_remote_copy(
             src_ref=src,
@@ -203,16 +213,20 @@
 
     sides = ((gx, 4, "gx"), (gy, 4, "gy"), (gz, NS, "gz"))
 
-    def layers(array, zs, zr):
+    def layers(array, zs, zr, halved):
+        size = B // 2 if halved else B
+        lower, upper = pl.ds(1, size), pl.ds(1 + B - size, size)
+        z_lower, z_upper = pl.ds(0, size), pl.ds(B - size, size)
         return (
-            ((array.at[B, inner], array.at[0, inner]), (array.at[1, inner], array.at[B + 1, inner])),
-            ((array.at[inner, B], array.at[inner, 0]), (array.at[inner, 1], array.at[inner, B + 1])),
-            ((zs.at[1], zr.at[0]), (zs.at[0], zr.at[1])),
+            ((array.at[B, lower], array.at[0, lower]), (array.at[1, upper], array.at[B + 1, upper])),
+            ((array.at[lower, B], array.at[lower, 0]), (array.at[upper, 1], array.at[upper, B + 1])),
+            ((zs.at[1, z_lower], zr.at[0, z_lower]), (zs.at[0, z_upper], zr.at[1, z_upper])),
         )
 
-    def halo_copies(array, zs, zr, send, recv):
+    def halo_copies(array, zs, zr, send, recv, halved=False):
         copies = []
-        for axis, ((place, extent, name), pairs) in enumerate(zip(sides, layers(array, zs, zr))):
+        parts = layers(array, zs, zr, halved)
+        for axis, ((place, extent, name), pairs) in enumerate(zip(sides, parts)):
             for way, (src, dst) in enumerate(pairs):
                 there = place + 1 if way == 0 else place - 1
                 exists = place < extent - 1 if way == 0 else place > 0
@@ -248,7 +262,7 @@
 
     hh = halo_copies(half, hzsend, hzrecv, hh_s, hh_r)
     halos = [
-        halo_copies(field.at[k], zsend.at[k], zrecv.at[k], halo_s.at[k], halo_r.at[k])
+        halo_copies(field.at[k], zsend.at[k], zrecv.at[k], halo_s.at[k], halo_r.at[k], k == 1)
         for k in range(2)
     ]
 
@@ -291,55 +305,62 @@
 
         each(1, NS, body)
 
-    def gath_copies(k):
-        direct = [
-            remote(gath.at[k, gz], gath.at[k, gz], gath_s.at[k, 0], gath_r.at[k, gz], {"gz": mate})
+    plus, minus, far = [lax.rem(chip + j, 4) * 2 + core for j in (1, 3, 2)]
+
+    def half_block(k, slot, part, sem, to):
+        ref = gath.at[k, slot, pl.ds(part * 128, 128)]
+        return remote(ref, ref, gath_s.at[k, sem], gath_r.at[k, slot, part], {"gz": to})
+
+    def gath_own(k):
+        return [
+            half_block(k, gz, part, sem, to)
+            for sem, (part, to) in enumerate(
+                ((0, plus), (1, minus), (1, plus), (0, minus), (0, mate), (1, mate))
+            )
         ]
-        passed, arrivals = [], []
-        for i, j in enumerate((1, 3, 2)):
-            peer = lax.rem(chip + j, 4) * 2 + core
-            direct.append(
-                remote(
-                    gath.at[k, gz],
-                    gath.at[k, gz],
-                    gath_s.at[k, 1 + i],
-                    gath_r.at[k, gz],
-                    {"gz": peer},
+
+    def gath_onward(k):
+        return [
+            half_block(k, slot, part, 6 + sem, to)
+            for sem, (slot, part, to) in enumerate(
+                (
+                    (minus, 0, plus),
+                    (plus, 1, minus),
+                    (minus, 0, mate),
+                    (plus, 1, mate),
+                    (minus, 1, mate),
+                    (plus, 0, mate),
+                    (far, 0, mate),
+                    (far, 1, mate),
                 )
             )
-            back = lax.rem(chip + j, 4) * 2 + core
-            arrivals.append(
-                remote(
-                    gath.at[k, back],
-                    gath.at[k, back],
-                    gath_s.at[k, 4 + i],
-                    gath_r.at[k, back],
-                    {"gz": mate},
-                )
-            )
-            other = lax.rem(chip + j, 4) * 2 + 1 - core
-            passed.append(
-                remote(
-                    gath.at[k, other],
-                    gath.at[k, other],
-                    gath_s.at[k, 4 + i],
-                    gath_r.at[k, other],
-                    {"gz": mate},
-                )
-            )
-        from_mate = remote(
-            gath.at[k, mate], gath.at[k, mate], gath_s.at[k, 0], gath_r.at[k, mate], {"gz": mate}
-        )
-        return direct, arrivals, passed, from_mate
+        ]
+
+    def gath_wait(k, slot):
+        for part in range(2):
+            half_block(k, slot, part, 0, mate).wait_recv()
+
+    def near_block(k, slot, first=False):
+        columns = pl.ds(pl.multiple_of(slot * 256, 256), 256)
+        value = dot3(col[:, columns], gath[k, slot])
+        near[...] = value if first else near[...] + value
 
     def leaf_products(src, k, first, last):
         def body(b):
             u_high, u_low = split(src[box_of(b, 0)].reshape(512, N))
             if k == 0:
-                pltpu.make_async_copy(leaf_hbm.at[b], leaf.at[b], loc_sem.at[9 + b]).wait()
-                high, low = split(leaf[b])
+                slot = lax.rem(b, 4)
+                pltpu.make_async_copy(leaf_hbm.at[b], leaf.at[slot], loc_sem.at[9 + b]).wait()
+                high, low = split(leaf[slot])
                 leaf_hi[b] = high
                 leaf_lo[b] = low
+
+                @pl.when(b < 4)
+                def _():
+                    pltpu.make_async_copy(
+                        leaf_hbm.at[b + 4], leaf.at[slot], loc_sem.at[13 + b]
+                    ).start()
+
             else:
                 high, low = leaf_hi[b], leaf_lo[b]
             total = mm(high, u_high) + mm(high, u_low) + mm(low, u_high)
@@ -347,11 +368,13 @@
 
         each(first, last, body)
 
-    def precondition(src, k, middle, last_step):
+    def precondition(src, k, middle, later):
         restrict_all(src, k)
+        if k == 0:
+            pl.semaphore_wait(barrier, NS - 1 + NPQ - 1)
         rs_start(k)
-        direct, arrivals, passed, from_mate = gath_copies(k)
-        for copy in direct:
+        own, onward = gath_own(k), gath_onward(k)
+        for copy in own:
             copy.start()
         middle()
         leaf_products(src, k, 0, 3)
@@ -361,31 +384,42 @@
             total = total + rs[k, i]
         ag[k, pq] = total
         plane_start(ag, ag_s, ag_r, k)
-        leaf_products(src, k, 3, 6)
-        plane_wait(ag, ag_s, ag_r, k)
+        leaf_products(src, k, 3, 5)
+        for i in (0, 1):
+            onward[2 + i].wait_recv()
+            onward[i].start()
+            onward[2 + i].start()
         if k == 0:
             loads[6].wait()
+        leaf_products(src, k, 5, 6)
+        plane_wait(ag, ag_s, ag_r, k)
         tops = jnp.concatenate([ag[k, i] for i in range(NPQ)], axis=1)
         tg[k, gz] = dot3(tops, top[...], mm_nt)
         column_start(tg, tg_s, tg_r, k)
-        for copy in arrivals:
-            copy.wait_recv()
-            copy.start()
+        for i in (4, 5):
+            onward[i].wait_recv()
+            onward[i].start()
         leaf_products(src, k, 6, 8)
+        for i in (6, 7):
+            onward[i].wait_recv()
+            onward[i].start()
         if k == 0:
             loads[5].wait()
             loads[7].wait()
         dev_out[...] = dot3(dev[...], dev_in[...])
-        from_mate.wait_recv()
-        for copy in passed:
-            copy.wait_recv()
-        near = dot3(col[...], gath[k].reshape(NS * 256, N))
+        later()
+        near_block(k, gz, True)
+        for slot in (minus, plus, far):
+            near_block(k, slot)
+        for base in (gz, minus, plus, far):
+            slot = base + mate - gz
+            gath_wait(k, slot)
+            near_block(k, slot)
         column_wait(tg, tg_s, tg_r, k)
-        column_out = near + dot3(col_v[...], tg[k].reshape(N, 128), mm_nt)
+        column_out = near[...] + dot3(col_v[...], tg[k].reshape(N, 128), mm_nt)
         dev_out[...] += dot3(dev_v[...], column_out)
-        for copy in direct + arrivals:
+        for copy in own + onward:
             copy.wait_send()
-        last_step()
 
     def lift_boxes(k, finish):
         def body(b):
@@ -397,56 +431,92 @@
 
         each(0, 8, body)
 
+    def twice(value):
+        return jnp.concatenate([value, value], axis=1)
+
     def stencil(k, use):
-        rows = lax.broadcasted_iota(jnp.int32, (B, N), 0)
+        rows = lax.broadcasted_iota(jnp.int32, (B, 128), 0)
         first, last = rows == 0, rows == B - 1
-        first_h, last_h = first[:, :128], last[:, :128]
-
-        def shifted(value, low, high, is_first, is_last):
-            up = jnp.where(is_last, high, pltpu.roll(value, B - 1, 0))
-            down = jnp.where(is_first, low, pltpu.roll(value, 1, 0))
-            return up, down
 
         def body(x, carry):
             energy, curve = carry
+            has_low = jnp.where(x > 0, 1.0, 0.0).astype(F32)
+            has_high = jnp.where(x < B - 1, 1.0, 0.0).astype(F32)
+            x_low, x_high = jnp.maximum(x, 1), jnp.minimum(x + 2, B)
             for y in range(B):
                 v = field[k, x + 1, y + 1]
                 h = half[x + 1, y + 1]
-                v_up, v_down = shifted(
-                    v, zrecv[k, 0, x, y : y + 1, :], zrecv[k, 1, x, y : y + 1, :], first, last
+                if k == 1:
+                    face_up = jnp.where(last, 0.0, h + pltpu.roll(h, B - 1, 0))
+                    face_xh = (h + half[x + 2, y + 1]) * has_high
+                    applied = (
+                        twice(0.5 * react[x, y]) * v
+                        - twice(face_xh) * field[k, x_high, y + 1]
+                        - twice(face_up) * pltpu.roll(v, B - 1, 0)
+                    )
+                    if y < B - 1:
+                        face_yh = h + half[x + 1, y + 2]
+                        applied = applied - twice(face_yh) * field[k, x + 1, y + 2]
+                    energy = energy + use(x, y, None) * v
+                    curve = curve + v * applied
+                    continue
+                low, high = hzrecv[0, x, y : y + 1, :], hzrecv[1, x, y : y + 1, :]
+                face_up = h + jnp.where(last, high, pltpu.roll(h, B - 1, 0))
+                face_down = h + jnp.where(first, low, pltpu.roll(h, 1, 0))
+                face_xl, face_xh = h + half[x, y + 1], h + half[x + 2, y + 1]
+                face_yl = h + half[x + 1, y] if y == 0 else face_yh
+                face_yh = h + half[x + 1, y + 2]
+                total = react[x, y] + face_up + face_down + face_xl + face_xh + face_yl + face_yh
+                react[x, y] = total
+                applied = (
+                    twice(total) * v
+                    - twice(face_xl * has_low) * field[k, x_low, y + 1]
+                    - twice(face_xh * has_high) * field[k, x_high, y + 1]
+                    - twice(jnp.where(last, 0.0, face_up)) * pltpu.roll(v, B - 1, 0)
+                    - twice(jnp.where(first, 0.0, face_down)) * pltpu.roll(v, 1, 0)
                 )
-                h_up, h_down = shifted(
-                    h, hzrecv[0, x, y : y + 1, :], hzrecv[1, x, y : y + 1, :], first_h, last_h
-                )
-                total = react[x, y]
-                pairs = (
-                    (half[x, y + 1], field[k, x, y + 1]),
-                    (half[x + 2, y + 1], field[k, x + 2, y + 1]),
-                    (half[x + 1, y], field[k, x + 1, y]),
-                    (half[x + 1, y + 2], field[k, x + 1, y + 2]),
-                    (h_up, v_up),
-                    (h_down, v_down),
-                )
-                off = None
-                for other, value in pairs:
-                    face = h + other
-                    total = total + face
-                    part = jnp.concatenate([face, face], axis=1) * value
-                    off = part if off is None else off + part
-                applied = jnp.concatenate([total, total], axis=1) * v - off
-                residual = use(x, y, applied)
-                energy = energy + residual * v
+                if y > 0:
+                    applied = applied - twice(face_yl) * field[k, x + 1, y]
+                if y < B - 1:
+                    applied = applied - twice(face_yh) * field[k, x + 1, y + 2]
+                energy = energy + use(x, y, applied) * v
                 curve = curve + v * applied
             return energy, curve
 
         zero = jnp.zeros((B, N), F32)
         return lax.fori_loop(0, B, body, (zero, zero))
 
+    def outer_terms(k, curve):
+        def body(i, total):
+            for side in range(2):
+                at = i + B // 2 * side if k == 1 else i
+                edge, beyond = (1, 0) if side == 0 else (B, B + 1)
+                part = twice(half[edge, at + 1] + half[beyond, at + 1]) * field[k, beyond, at + 1]
+                total = total + part * field[k, edge, at + 1]
+                if k == 0:
+                    image[edge - 1, at] -= part
+                part = twice(half[at + 1, edge] + half[at + 1, beyond]) * field[k, at + 1, beyond]
+                total = total + part * field[k, at + 1, edge]
+                if k == 0:
+                    image[at, edge - 1] -= part
+                part = twice(hzsend[side, at] + hzrecv[side, at]) * zrecv[k, side, at]
+                total = total + part * zsend[k, side, at]
+                if k == 0:
+                    image[at, :, edge - 1, :] -= part
+            return total
+
+        count = B // 2 if k == 1 else B
+        total = lax.fori_loop(0, count, body, jnp.zeros((B, N), F32))
+        return 2.0 * (curve - total) if k == 1 else curve - total
+
     def ar_first(k, energy, curve):
-        row = lax.broadcasted_iota(jnp.int32, (8, N), 0)
+        row = lax.broadcasted_iota(jnp.int32, (8, 128), 0)
         e = jnp.sum(energy, axis=0, keepdims=True)
         c = jnp.sum(curve, axis=0, keepdims=True)
-        ar1[k, gz] = jnp.where(row == 0, e, jnp.where(row == 1, c, 0.0))
+        packed = jnp.where(row == 3, c[:, 128:], 0.0)
+        for i, line in enumerate((e[:, :128], e[:, 128:], c[:, :128])):
+            packed = jnp.where(row == i, line, packed)
+        ar1[k, gz] = packed
         column_start(ar1, a1_s, a1_r, k)
 
     def ar_second(k):
@@ -462,20 +532,31 @@
         total = ar2[k, 0]
         for i in range(1, NPQ):
             total = total + ar2[k, i]
-        return total[0:1], total[1:2]
-
-    loads[1].wait()
+        lines = [total[i : i + 1] for i in range(4)]
+        return jnp.concatenate(lines[:2], axis=1), jnp.concatenate(lines[2:], axis=1)
+
+    for i in (1, 9, 10, 11):
+        loads[i].wait()
+    padded = jnp.concatenate([leaf_s[...], jnp.zeros((8, 64), jnp.int32)], axis=1).astype(F32)
+    numbers = padded.T[:64]
+    chosen_box = lax.broadcasted_iota(jnp.int32, (64, 8), 1)
+    places = lax.broadcasted_iota(jnp.int32, (64, 512), 1).astype(F32)
 
     def prepare(b):
-        high, low = split(leaf_v[b])
+        mine = jnp.sum(jnp.where(chosen_box == b, numbers, 0.0), axis=1, keepdims=True)
+        high, low = split(leaf_v[b] + jnp.where(places == mine, 1.0, 0.0))
         leaf_vt[b] = jnp.concatenate([high, low], axis=0)
         high, low = high.astype(F32), low.astype(F32)
         leaf_v3[b] = jnp.concatenate([high, high, low, jnp.zeros_like(low)], axis=0).T.astype(BF16)
 
     each(0, 8, prepare)
     loads[2].wait()
+    rows = lax.broadcasted_iota(jnp.int32, (512, 256), 0)
+    dev_v[...] += jnp.where(rows == dev_s[...], 1.0, 0.0)
     dev_vt[...] = dev_v[...].T
     loads[3].wait()
+    rows = lax.broadcasted_iota(jnp.int32, (256, 128), 0) + gz * 256
+    col_v[...] += jnp.where(rows == col_s[...], 1.0, 0.0)
     col_vt[...] = col_v[...].T
     loads[0].wait()
 
@@ -484,6 +565,21 @@
 
     def send_halves():
         loads[4].wait()
+        loads[8].wait()
+        diagonal = lax.broadcasted_iota(jnp.int32, (B, B), 0) == lax.broadcasted_iota(
+            jnp.int32, (B, B), 1
+        )
+
+        def spread(line):
+            value = jnp.sum(jnp.where(diagonal, line, 0.0), axis=1, keepdims=True)
+            return jnp.broadcast_to(value, (B, 128))
+
+        def body(x):
+            for y in range(B):
+                half[x + 1, y + 1] = 0.5 * spread(cond_raw[x, y : y + 1, :])
+                react[x, y] = spread(react_raw[x, y : y + 1, :])
+
+        each(0, B, body)
         pack_z(half, hzsend)
         halo_start(hh)
 
@@ -496,18 +592,17 @@
     pack_z(field.at[0], zsend.at[0])
     halo_start(halos[0])
     halo_wait(hh)
-    loads[8].wait()
-    halo_wait(halos[0])
 
     def use_first(x, y, applied):
         image[x, y] = applied
         return rhs[x, y]
 
     energy, curve = stencil(0, use_first)
+    halo_wait(halos[0])
+    curve = outer_terms(0, curve)
     ar_first(0, energy, curve)
 
-    precondition(image, 1, lambda: None, lambda: None)
-    ar_second(0)
+    precondition(image, 1, lambda: ar_second(0), lambda: None)
     energy0, curve0 = ar_third(0)
     step0 = energy0 / curve0
 
@@ -517,12 +612,13 @@
     lift_boxes(1, subtract)
     pack_z(field.at[1], zsend.at[1])
     halo_start(halos[1])
-    halo_wait(halos[1])
 
     def use_second(x, y, applied):
         return rhs[x, y] - step0 * image[x, y]
 
     energy, curve = stencil(1, use_second)
+    halo_wait(halos[1])
+    curve = outer_terms(1, curve)
     ar_first(1, energy, curve)
     ar_second(1)
     energy1, curve1 = ar_third(1)
@@ -558,30 +654,20 @@
     column_skeleton,
     top_factor,
 ):
-    def onehot(skeleton, rows, first=0):
-        numbers = lax.broadcasted_iota(jnp.int32, (rows, 1), 0) + first
-        return (numbers == skeleton[None, :]).astype(F32)
-
-    wide = (B, B, B, 128)
-    half = jnp.broadcast_to((0.5 * conductivity)[..., None], wide)
-    react = jnp.broadcast_to(reaction[..., None], wide)
-    skeleton = leaf_skeleton.reshape(8, 64)
-    leaf_v = jnp.swapaxes(leaf_weight.reshape(8, 512, 64), 1, 2) + (
-        skeleton[..., None] == lax.broadcasted_iota(jnp.int32, (1, 1, 512), 2)
-    ).astype(F32)
-    dev_v = device_weight[0, 0, 0] + onehot(device_skeleton[0, 0, 0], 512)
-    start = lax.axis_index("gz") * 256
-    col_v = lax.dynamic_slice_in_dim(column_weight[0, 0], start, 256, 0) + onehot(
-        column_skeleton[0, 0], 256, start
-    )
+    leaf_w = jnp.swapaxes(leaf_weight.reshape(8, 512, 64), 1, 2)
     any_space = pl.BlockSpec(memory_space=pl.ANY)
     dma = pltpu.SemaphoreType.DMA
     vm = pltpu.VMEM
     scratch = [
         vm((B, B, B, N), F32),
+        vm((B, B, B), F32),
+        vm((B, B, B), F32),
+        vm((8, 64), jnp.int32),
+        vm((1, 256), jnp.int32),
+        vm((1, 128), jnp.int32),
         vm((B + 2, B + 2, B, 128), F32),
         vm((B, B, B, 128), F32),
-        vm((8, 512, 512), F32),
+        vm((4, 512, 512), F32),
         vm((8, 512, 512), BF16),
         vm((8, 512, 512), BF16),
         vm((8, 64, 512), F32),
@@ -600,19 +686,20 @@
         vm((512, N), F32),
         vm((2, N, 128), F32),
         vm((2, NS, 256, N), F32),
+        vm((256, N), F32),
         vm((2, NS, PIECE, 128), F32),
         vm((2, NPQ, PIECE, 128), F32),
         vm((2, NS, PIECE, 128), F32),
-        vm((2, NS, 8, N), F32),
-        vm((2, NPQ, 8, N), F32),
+        vm((2, NS, 8, 128), F32),
+        vm((2, NPQ, 8, 128), F32),
         vm((2, 2, B, B, N), F32),
         vm((2, 2, B, B, N), F32),
         vm((2, B, B, 128), F32),
         vm((2, B, B, 128), F32),
-        dma((17,)),
+        dma((20,)),
         dma((B,)),
-        dma((2, NS)),
-        dma((2, NS)),
+        dma((2, 14)),
+        dma((2, NS, 2)),
         dma((2, NS)),
         dma((2, NS)),
         dma((2, NPQ)),
@@ -631,7 +718,7 @@
     return pl.pallas_call(
         kernel,
         out_shape=jax.ShapeDtypeStruct((B, B, B, N), F32),
-        in_specs=[any_space] * 10,
+        in_specs=[any_space] * 13,
         out_specs=any_space,
         scratch_shapes=scratch,
         compiler_params=pltpu.CompilerParams(
@@ -640,14 +727,17 @@
         name="cg",
     )(
         right_side,
-        half,
-        react,
+        conductivity,
+        reaction,
         leaf_factor.reshape(8, 512, 512),
-        leaf_v,
+        leaf_w,
+        leaf_skeleton.reshape(8, 64),
         device_factor[0, 0, 0],
-        dev_v,
+        device_weight[0, 0, 0],
+        device_skeleton.reshape(1, 256),
         column_factor[0, 0],
-        col_v,
+        column_weight[0, 0],
+        column_skeleton.reshape(1, 128),
         top_factor,
     )
 

time: 116 us -> 84.3 us (0.73)
  Pallas kernels: 99.8 us -> 79.4 us
  other arithmetic: 6.9 us -> 0 us
  local copies, waits for them, and re-layouts: 8.66 us -> 4.81 us
    pallas_call x1, Pallas kernels: 99.8 us -> 79.4 us  [local(): pl.pallas_call(kernel, out_shape=jax.ShapeDtypeStruct((B, B, B, N), F32),...]
    add x4 -> x0, other arithmetic: 5.99 us -> none  [the longest x1 2.4 us: local(): jnp.swapaxes(leaf_weight.reshape(8, 512, 64), 1, 2)]
    broadcast_in_dim x2 -> x0, local copies, waits for them, and re-layouts: 3.85 us -> none  [the longest x1 1.93 us: local(): react = jnp.broadcast_to(reaction[..., None], wide)]
    unnamed x3 -> x1, local copies, waits for them, and re-layouts: 4.81 us -> 4.81 us
where the time goes in v1:
time: 84.3 us; the launch traced here: 84.2 us
  Pallas kernels  79.4 us (94%)
  local copies, waits for them, and re-layouts  4.81 us (6%)
    pallas_call x1, Pallas kernels, local(): pl.pallas_call(kernel, out_shape=jax.ShapeDtypeStruct((B, B, B, N), F32),...  79.4 us
    unnamed x1, local copies, waits for them, and re-layouts  4.81 us

profile of v1, /device:TPU:1, one launch (start us, length us, event | category | flops | bytes accessed | tf_op | source)
XLA Modules:
  0.0 84.2 jit_solution(17409038371184583905)
XLA Ops:
  0.0 79.4 %cg.1 = f32[16,16,16,256]{3,2,1,0:T(8,128)} custom-call(f32[16,16,16,256]{3,2,1,0:T(8,128)} %rhs_hbm.1, f32[16,16,16]{2,1,0:T(8,128)} %cond_hbm.1, f32[16,16,16]{2,1,0:T(8,128)} %react_hbm.1, f32[8,512,512]{2,1,0:T(8,128)} %bitcast.11, f32[8,64,512]{2,1,0:T(8,128)} %bitcast.13, s32[8,64]{1,0:T(8,128)} %bitcast.17, f32[512,512]{1,0:T(8,128)} %bitcast.14, ...), custom_call_target="tpu_custom_call" | custom-call | tf_op jit(solution)/shard_map/cg/pallas_call | solution.py:718
  79.4 4.8 %copy.15 = f32[16,16,16,256]{3,2,1,0:T(8,128)} copy(f32[16,16,16,256]{3,2,1,0:T(8,128)} %cg.1) | data formatting | bytes 8388608

commit v2 on v1

--- a/solution.py
+++ b/solution.py
@@ -85,7 +85,11 @@
     col,
     col_v,
     col_vt,
+    up_c,
+    down_c,
     top,
+    top_hi,
+    top_lo,
     field,
     image,
     dev_in,
@@ -127,14 +131,19 @@
     mate = gz + 1 - 2 * core
     inner = pl.ds(1, B)
 
-    def plane_id(peer):
-        return {"gx": lax.div(peer, 4), "gy": lax.rem(peer, 4)}
+    column_peers = [
+        lax.rem(chip + j, 4) * 2 + (1 - core if other else core)
+        for j, other in ((2, 0), (2, 1), (1, 0), (1, 1), (3, 0), (3, 1), (0, 1))
+    ]
+    offsets = [(i, j) for i in range(4) for j in range(4) if i or j]
+    offsets.sort(key=lambda o: -min(o[0], 4 - o[0]) - min(o[1], 4 - o[1]))
+    plane_peers = [(lax.rem(gx + i, 4), lax.rem(gy + j, 4)) for i, j in offsets]
 
     def local(i, src, dst):
         return pltpu.make_async_copy(src, dst, loc_sem.at[i])
 
     loads = [
-        local(0, rhs_hbm, rhs),
+        local(0, rhs_hbm.at[pl.ds(0, 8)], rhs.at[pl.ds(0, 8)]),
         local(1, leaf_w_hbm, leaf_v),
         local(2, dev_w_hbm, dev_v),
         local(3, col_w_hbm.at[pl.ds(pl.multiple_of(gz * 256, 256), 256)], col_v),
@@ -146,25 +155,19 @@
         local(17, leaf_s_hbm, leaf_s),
         local(18, dev_s_hbm, dev_s),
         local(19, col_s_hbm, col_s),
+        local(20, rhs_hbm.at[pl.ds(8, 8)], rhs.at[pl.ds(8, 8)]),
     ]
     leaf_loads = [local(9 + b, leaf_hbm.at[b], leaf.at[b]) for b in range(4)]
-    for copy in loads[9:] + loads[1:4] + loads[:1] + leaf_loads[:2] + loads[4:9] + leaf_loads[2:]:
+    for copy in loads[9:12] + loads[1:4] + loads[:1] + loads[12:]:
         copy.start()
 
     barrier = pltpu.get_barrier_semaphore()
 
-    def greet_column(d):
-        pl.semaphore_signal(
-            barrier, inc=1, device_id={"gz": lax.rem(gz + d, NS)}, device_id_type=MESH
-        )
-
-    def greet_plane(d):
-        pl.semaphore_signal(
-            barrier, inc=1, device_id=plane_id(lax.rem(pq + d, NPQ)), device_id_type=MESH
-        )
-
-    each(1, NS, greet_column)
-    each(1, NPQ, greet_plane)
+    for x, y in plane_peers:
+        pl.semaphore_signal(barrier, inc=1, device_id={"gx": x, "gy": y}, device_id_type=MESH)
+    for peer in column_peers:
+        pl.semaphore_signal(barrier, inc=1, device_id={"gz": peer}, device_id_type=MESH)
+
     def remote(src, dst, send, recv, device):
         return pltpu.make_async_remote_copy(
             src_ref=src,
@@ -176,40 +179,42 @@
         )
 
     def column_start(buf, send, recv, k):
-        def body(d):
-            peer = lax.rem(gz + d, NS)
+        def body(peer):
             remote(
                 buf.at[k, gz], buf.at[k, gz], send.at[k, peer], recv.at[k, gz], {"gz": peer}
             ).start()
 
-        each(1, NS, body)
+        for peer in column_peers:
+            body(peer)
 
     def column_wait(buf, send, recv, k):
-        def body(d):
-            peer = lax.rem(gz + d, NS)
+        def body(peer):
             remote(
                 buf.at[k, gz], buf.at[k, peer], send.at[k, peer], recv.at[k, peer], {"gz": peer}
             ).wait()
 
-        each(1, NS, body)
+        for peer in column_peers:
+            body(peer)
 
     def plane_start(buf, send, recv, k):
-        def body(d):
-            peer = lax.rem(pq + d, NPQ)
+        def body(x, y):
+            peer = x * 4 + y
             remote(
-                buf.at[k, pq], buf.at[k, pq], send.at[k, peer], recv.at[k, pq], plane_id(peer)
+                buf.at[k, pq], buf.at[k, pq], send.at[k, peer], recv.at[k, pq], {"gx": x, "gy": y}
             ).start()
 
-        each(1, NPQ, body)
+        for x, y in plane_peers:
+            body(x, y)
 
     def plane_wait(buf, send, recv, k):
-        def body(d):
-            peer = lax.rem(pq + d, NPQ)
+        def body(x, y):
+            peer = x * 4 + y
             remote(
-                buf.at[k, pq], buf.at[k, peer], send.at[k, peer], recv.at[k, peer], plane_id(peer)
+                buf.at[k, pq], buf.at[k, peer], send.at[k, peer], recv.at[k, peer], {"gx": x, "gy": y}
             ).wait()
 
-        each(1, NPQ, body)
+        for x, y in plane_peers:
+            body(x, y)
 
     sides = ((gx, 4, "gx"), (gy, 4, "gy"), (gz, NS, "gz"))
 
@@ -273,15 +278,21 @@
             total = both[:64] + both[64:] + mm(leaf_vt[b, :64], u_low)
             dev_in[pl.ds(pl.multiple_of(b * 64, 64), 64), :] = total
 
-        each(0, 8, leaf_box)
-        device_up = dot3(dev_vt[...], dev_in[...])
-        gath[k, gz] = device_up
-        up_t[k] = dot3(col_vt[...], device_up).T
+        if k == 0:
+            loads[0].wait()
+            loads[4].start()
+            loads[8].start()
+        each(0, 4, leaf_box)
+        if k == 0:
+            loads[12].wait()
+            for copy in leaf_loads[:2] + loads[6:7] + leaf_loads[2:] + loads[5:6] + loads[7:8]:
+                copy.start()
+        each(4, 8, leaf_box)
+        up_t[k] = dot3(up_c[...], dev_in[...]).T
         rs[k, gz] = up_t[k, pl.ds(pl.multiple_of(gz * PIECE, PIECE), PIECE), :]
 
     def rs_start(k):
-        def body(d):
-            peer = lax.rem(gz + d, NS)
+        def body(peer):
             remote(
                 up_t.at[k, pl.ds(pl.multiple_of(peer * PIECE, PIECE), PIECE)],
                 rs.at[k, gz],
@@ -290,11 +301,11 @@
                 {"gz": peer},
             ).start()
 
-        each(1, NS, body)
+        for peer in column_peers:
+            body(peer)
 
     def rs_wait(k):
-        def body(d):
-            peer = lax.rem(gz + d, NS)
+        def body(peer):
             remote(
                 up_t.at[k, pl.ds(pl.multiple_of(peer * PIECE, PIECE), PIECE)],
                 rs.at[k, peer],
@@ -303,7 +314,8 @@
                 {"gz": peer},
             ).wait()
 
-        each(1, NS, body)
+        for peer in column_peers:
+            body(peer)
 
     plus, minus, far = [lax.rem(chip + j, 4) * 2 + core for j in (1, 3, 2)]
 
@@ -373,6 +385,7 @@
         if k == 0:
             pl.semaphore_wait(barrier, NS - 1 + NPQ - 1)
         rs_start(k)
+        gath[k, gz] = dot3(dev_vt[...], dev_in[...])
         own, onward = gath_own(k), gath_onward(k)
         for copy in own:
             copy.start()
@@ -391,10 +404,14 @@
             onward[2 + i].start()
         if k == 0:
             loads[6].wait()
+            top_hi[...], top_lo[...] = split(top[...])
         leaf_products(src, k, 5, 6)
         plane_wait(ag, ag_s, ag_r, k)
         tops = jnp.concatenate([ag[k, i] for i in range(NPQ)], axis=1)
-        tg[k, gz] = dot3(tops, top[...], mm_nt)
+        high, low = split(tops)
+        rows = jnp.concatenate([high, low], axis=0)
+        both = mm_nt(rows, top_hi[...])
+        tg[k, gz] = both[:PIECE] + both[PIECE:] + mm_nt(high, top_lo[...])
         column_start(tg, tg_s, tg_r, k)
         for i in (4, 5):
             onward[i].wait_recv()
@@ -415,9 +432,9 @@
             slot = base + mate - gz
             gath_wait(k, slot)
             near_block(k, slot)
+        dev_out[...] += dot3(dev_v[...], near[...])
         column_wait(tg, tg_s, tg_r, k)
-        column_out = near[...] + dot3(col_v[...], tg[k].reshape(N, 128), mm_nt)
-        dev_out[...] += dot3(dev_v[...], column_out)
+        dev_out[...] += dot3(down_c[...], tg[k].reshape(N, 128), mm_nt)
         for copy in own + onward:
             copy.wait_send()
 
@@ -558,7 +575,7 @@
     rows = lax.broadcasted_iota(jnp.int32, (256, 128), 0) + gz * 256
     col_v[...] += jnp.where(rows == col_s[...], 1.0, 0.0)
     col_vt[...] = col_v[...].T
-    loads[0].wait()
+    up_c[...] = dot3(col_vt[...], dev_vt[...])
 
     for copies in [hh] + halos:
         halo_zero(copies)
@@ -582,6 +599,7 @@
         each(0, B, body)
         pack_z(half, hzsend)
         halo_start(hh)
+        down_c[...] = dot3(dev_v[...], col_v[...])
 
     precondition(rhs, 0, send_halves, lambda: None)
 
@@ -679,7 +697,11 @@
         vm((256, 2048), F32),
         vm((256, 128), F32),
         vm((128, 256), F32),
+        vm((128, 512), F32),
+        vm((512, 128), F32),
         vm((128, 2048), F32),
+        vm((128, 2048), BF16),
+        vm((128, 2048), BF16),
         vm((2, B + 2, B + 2, B, N), F32),
         vm((B, B, B, N), F32),
         vm((512, N), F32),
@@ -696,7 +718,7 @@
         vm((2, 2, B, B, N), F32),
         vm((2, B, B, 128), F32),
         vm((2, B, B, 128), F32),
-        dma((20,)),
+        dma((21,)),
         dma((B,)),
         dma((2, 14)),
         dma((2, NS, 2)),

time: 84.3 us -> 81.6 us (0.968)
  Pallas kernels: 79.4 us -> 76.7 us
    pallas_call x1, Pallas kernels: 79.4 us -> 76.7 us  [local(): pl.pallas_call(kernel, out_shape=jax.ShapeDtypeStruct((B, B, B, N), F32),...]
where the time goes in v2:
time: 81.6 us; the launch traced here: 81.5 us
  Pallas kernels  76.7 us (94%)
  local copies, waits for them, and re-layouts  4.81 us (6%)
    pallas_call x1, Pallas kernels, local(): pl.pallas_call(kernel, out_shape=jax.ShapeDtypeStruct((B, B, B, N), F32),...  76.7 us
    unnamed x1, local copies, waits for them, and re-layouts  4.81 us

profile of v2, /device:TPU:1, one launch (start us, length us, event | category | flops | bytes accessed | tf_op | source)
XLA Modules:
  0.0 81.5 jit_solution(15523410120277741921)
XLA Ops:
  0.0 76.7 %cg.1 = f32[16,16,16,256]{3,2,1,0:T(8,128)} custom-call(f32[16,16,16,256]{3,2,1,0:T(8,128)} %rhs_hbm.1, f32[16,16,16]{2,1,0:T(8,128)} %cond_hbm.1, f32[16,16,16]{2,1,0:T(8,128)} %react_hbm.1, f32[8,512,512]{2,1,0:T(8,128)} %bitcast.11, f32[8,64,512]{2,1,0:T(8,128)} %bitcast.13, s32[8,64]{1,0:T(8,128)} %bitcast.17, f32[512,512]{1,0:T(8,128)} %bitcast.14, ...), custom_call_target="tpu_custom_call" | custom-call | tf_op jit(solution)/shard_map/cg/pallas_call | solution.py:740
  76.7 4.8 %copy.15 = f32[16,16,16,256]{3,2,1,0:T(8,128)} copy(f32[16,16,16,256]{3,2,1,0:T(8,128)} %cg.1) | data formatting | bytes 8388608

commit v3 on v2

--- a/solution.py
+++ b/solution.py
@@ -187,11 +187,15 @@
         for peer in column_peers:
             body(peer)
 
-    def column_wait(buf, send, recv, k):
+    def column_wait(buf, send, recv, k, sent=False):
         def body(peer):
-            remote(
+            copy = remote(
                 buf.at[k, gz], buf.at[k, peer], send.at[k, peer], recv.at[k, peer], {"gz": peer}
-            ).wait()
+            )
+            if sent:
+                copy.wait_send()
+            else:
+                copy.wait_recv()
 
         for peer in column_peers:
             body(peer)
@@ -206,12 +210,16 @@
         for x, y in plane_peers:
             body(x, y)
 
-    def plane_wait(buf, send, recv, k):
+    def plane_wait(buf, send, recv, k, sent=False):
         def body(x, y):
             peer = x * 4 + y
-            remote(
+            copy = remote(
                 buf.at[k, pq], buf.at[k, peer], send.at[k, peer], recv.at[k, peer], {"gx": x, "gy": y}
-            ).wait()
+            )
+            if sent:
+                copy.wait_send()
+            else:
+                copy.wait_recv()
 
         for x, y in plane_peers:
             body(x, y)
@@ -255,7 +263,6 @@
 
     def halo_wait(copies):
         for copy, exists, arrives, _ in copies:
-            pl.when(exists)(copy.wait_send)
             pl.when(arrives)(copy.wait_recv)
 
     def pack_z(array, zs):
@@ -304,15 +311,19 @@
         for peer in column_peers:
             body(peer)
 
-    def rs_wait(k):
+    def rs_wait(k, sent=False):
         def body(peer):
-            remote(
+            copy = remote(
                 up_t.at[k, pl.ds(pl.multiple_of(peer * PIECE, PIECE), PIECE)],
                 rs.at[k, peer],
                 rs_s.at[k, peer],
                 rs_r.at[k, peer],
                 {"gz": peer},
-            ).wait()
+            )
+            if sent:
+                copy.wait_send()
+            else:
+                copy.wait_recv()
 
         for peer in column_peers:
             body(peer)
@@ -379,6 +390,8 @@
             field[(k,) + box_of(b, 1)] = total.reshape(8, 8, 8, N)
 
         each(first, last, body)
+
+    unsent = []
 
     def precondition(src, k, middle, later):
         restrict_all(src, k)
@@ -435,8 +448,7 @@
         dev_out[...] += dot3(dev_v[...], near[...])
         column_wait(tg, tg_s, tg_r, k)
         dev_out[...] += dot3(down_c[...], tg[k].reshape(N, 128), mm_nt)
-        for copy in own + onward:
-            copy.wait_send()
+        unsent.extend(own + onward)
 
     def lift_boxes(k, finish):
         def body(b):
@@ -650,6 +662,17 @@
         pltpu.make_async_copy(image.at[x], out_hbm.at[x], out_sem.at[x]).start()
 
     each(0, B, write)
+    for copy in unsent:
+        copy.wait_send()
+    for k in range(2):
+        rs_wait(k, True)
+        plane_wait(ag, ag_s, ag_r, k, True)
+        column_wait(tg, tg_s, tg_r, k, True)
+        column_wait(ar1, a1_s, a1_r, k, True)
+        plane_wait(ar2, a2_s, a2_r, k, True)
+    for copies in [hh] + halos:
+        for copy, exists, _, _ in copies:
+            pl.when(exists)(copy.wait_send)
 
     def written(x):
         pltpu.make_async_copy(image.at[x], out_hbm.at[x], out_sem.at[x]).wait()

time: 81.6 us -> 81.5 us (level)
  no operation moved by 1% of the time
where the time goes in v3:
time: 81.5 us; the launch traced here: 81.4 us
  Pallas kernels  76.5 us (94%)
  local copies, waits for them, and re-layouts  4.81 us (6%)
    pallas_call x1, Pallas kernels, local(): pl.pallas_call(kernel, out_shape=jax.ShapeDtypeStruct((B, B, B, N), F32),...  76.5 us
    unnamed x1, local copies, waits for them, and re-layouts  4.81 us

profile of v3, /device:TPU:1, one launch (start us, length us, event | category | flops | bytes accessed | tf_op | source)
XLA Modules:
  0.0 81.4 jit_solution(18155071790467886290)
XLA Ops:
  0.0 76.5 %cg.1 = f32[16,16,16,256]{3,2,1,0:T(8,128)} custom-call(f32[16,16,16,256]{3,2,1,0:T(8,128)} %rhs_hbm.1, f32[16,16,16]{2,1,0:T(8,128)} %cond_hbm.1, f32[16,16,16]{2,1,0:T(8,128)} %react_hbm.1, f32[8,512,512]{2,1,0:T(8,128)} %bitcast.11, f32[8,64,512]{2,1,0:T(8,128)} %bitcast.13, s32[8,64]{1,0:T(8,128)} %bitcast.17, f32[512,512]{1,0:T(8,128)} %bitcast.14, ...), custom_call_target="tpu_custom_call" | custom-call | tf_op jit(solution)/shard_map/cg/pallas_call | solution.py:763
  76.5 4.8 %copy.15 = f32[16,16,16,256]{3,2,1,0:T(8,128)} copy(f32[16,16,16,256]{3,2,1,0:T(8,128)} %cg.1) | data formatting | bytes 8388608
